TPU v7x, 128 devices: a whole 4x4x4 slice. The times are simulated.
128 devices in a mesh: grp: 4 (over z), shard: 8 (over y_hi, x), tp: 4 (over y_lo, core).
Axes of the slice: x: 4, y: 4 (y_hi: 2, y_lo: 2; y = y_hi * 2 + y_lo), z: 4, core: 2. Of those that a mesh axis runs over, the one named last changes fastest.
Arguments:
- inner_weights: float32 [4, 2, 4096, 7168], P('grp', None, 'shard', 'tp'), may hold values from -6 to 6
- start_weights: float32 [2, 4096, 7168], P(None, 'shard', 'tp'), may hold values from -6 to 6
- momentum: float32 [2, 8, 4, 128, 4, 1792], P(None, None, None, ('grp', 'shard', 'tp')), may hold values from -6 to 6
Outputs:
- new_weights: float32 [2, 4096, 7168], P(None, 'shard', 'tp')
- new_momentum: float32 [2, 8, 4, 128, 4, 1792], P(None, None, None, ('grp', 'shard', 'tp'))
All inputs are finite; a program needn't handle non-finite values.
Results may differ from a plain program's by a relative error of at most 0.00002.
Values sent between devices are 32-bit elements; how exact they have to be, the bound alone decides.
A program may use at most 128 MiB of HBM per device.

v0:
```python
import jax
import jax.numpy as jnp
from jax import lax
from jax.sharding import PartitionSpec as P

OUTER_RATE = 0.7
MOMENTUM_COEF = 0.5


def body(inner_weights, start_weights, momentum):
    groups = lax.axis_size("grp")
    shards = lax.axis_size("shard")
    tp_size = lax.axis_size("tp")
    devices = groups * shards * tp_size
    row_count = start_weights.shape[1]
    col_count = start_weights.shape[2]
    q_rows = row_count // devices
    differ = start_weights - inner_weights[0]
    pieces = differ.reshape(2, devices, q_rows, col_count)
    landed = lax.all_to_all(pieces, ("grp", "shard", "tp"), split_axis=1, concat_axis=1, tiled=True)
    summed = jnp.sum(landed.reshape(2, groups, shards * tp_size, q_rows, col_count), axis=1)
    flat_diff = summed.reshape(2, shards, tp_size, 1, q_rows, col_count) / groups
    new_momentum = MOMENTUM_COEF * momentum + flat_diff
    flat_step = OUTER_RATE * (flat_diff + MOMENTUM_COEF * new_momentum)
    outgoing = flat_step.reshape(2, shards * tp_size, q_rows, col_count)
    own_part = lax.all_to_all(outgoing, ("shard", "tp"), split_axis=1, concat_axis=1, tiled=True)
    gathered = lax.all_gather(own_part, "grp", axis=1, tiled=True)
    new_weights = start_weights - gathered.reshape(2, row_count, col_count)
    return (new_weights, new_momentum)


def solution(mesh):
    in_specs = (
        P("grp", None, "shard", "tp"),
        P(None, "shard", "tp"),
        P(None, None, None, ("grp", "shard", "tp"), None, None),
    )
    out_specs = (P(None, "shard", "tp"), P(None, None, None, ("grp", "shard", "tp"), None, None))
    return jax.shard_map(body, mesh=mesh, in_specs=in_specs, out_specs=out_specs, check_vma=False)
```

profile of v0, /device:TPU:1, one launch (start us, length us, event | category | flops | bytes accessed | tf_op | source)
XLA Modules:
  0.0 274.8 jit_solution(16984734212106044562)
XLA Ops:
  7.2 0.0 all-gather.2.cloned.1.call-start
  7.2 9.1 %bitcast_subtract_fusion.1 = f32[2,512,1792]{2,1,0:T(8,128)} fusion(f32[2,512,1792]{2,1,0:T(8,128)} %param.4, f32[1,2,512,1792]{3,2,1,0:T(8,128)} %param.3), kind=kLoop, calls=%fused_computation.1 | loop fusion | flops 1835008 | bytes 22020096 | tf_op jit(solution)/shard_map/sub | solution.py:18
  16.3 11.7 %copy.12 = f32[2,512,1792]{2,0,1:T(2,128)} copy(f32[2,512,1792]{2,1,0:T(8,128)} %bitcast_subtract_fusion.1) | data formatting | bytes 14680064 | tf_op jit(solution)/shard_map/sub | solution.py:18
  28.0 5.0 %copy.13 = f32[2,128,4,1792]{3,2,0,1:T(4,128)S(1)} copy(f32[2,128,4,1792]{3,0,2,1:T(2,128)} %bitcast.9) | data formatting | bytes 14680064 | tf_op jit(solution)/shard_map/reshape | solution.py:19
  33.0 97.7 %all_to_all.10 = f32[2,128,4,1792]{3,2,0,1:T(4,128)} all-to-all(f32[2,128,4,1792]{3,2,0,1:T(4,128)S(1)} %copy.13), channel_id=1, replica_groups=mesh['grp'=4,'shard'=8,'tp'=4] {'grp','shard','tp'}, dimensions={1} | all-to-all | bytes 14680064 | tf_op jit(solution)/shard_map/all_to_all | solution.py:20
  130.7 4.9 %reduce_sum.9 = f32[2,32,4,1792]{3,2,0,1:T(4,128)S(1)} reduce(f32[2,4,32,4,1792]{4,3,0,2,1:T(4,128)} %bitcast.8, f32[]{:T(128)} %constant.1.clone.1), dimensions={1}, to_apply=%region_0.0 | reduce | flops 1376256 | bytes 9175044 | tf_op jit(solution)/shard_map/reduce_sum | solution.py:21
  135.6 0.0 copy-start
  135.6 0.4 broadcast_multiply_fusion
  136.0 1.1 copy-done
  137.1 2.2 add_multiply_fusion
  139.3 0.1 copy.16
  139.5 31.6 %all_to_all.11 = f32[2,32,4,1792]{3,2,0,1:T(4,128)} all-to-all(f32[2,32,4,1792]{3,2,0,1:T(4,128)S(1)} %bitcast.11), channel_id=1, replica_groups=mesh['grp'=4,'shard'=8,'tp'=4] {'shard','tp'}, dimensions={1} | all-to-all | bytes 3670016 | tf_op jit(solution)/shard_map/all_to_all | solution.py:26
  171.1 0.0 all-gather.2.cloned.1.call-update
  171.1 70.2 %all-gather.2.cloned.1.call-done = f32[2,128,4,1792]{3,2,0,1:T(4,128)} async-done(((f32[2,32,4,1792]{3,2,0,1:T(4,128)}), f32[2,128,4,1792]{3,2,0,1:T(4,128)}) %all-gather.2.cloned.1.call-update) | async-done | bytes 7340048 | tf_op jit(solution)/shard_map/all_gather | solution.py:27
  241.4 9.9 %copy.17 = f32[2,128,4,1792]{3,0,2,1:T(2,128)} copy(f32[2,128,4,1792]{3,2,0,1:T(4,128)} %all-gather.2.cloned.1.call-done) | data formatting | bytes 14680064 | tf_op jit(solution)/shard_map/all_gather | solution.py:27
  251.3 13.1 %bitcast_subtract_fusion = f32[2,512,1792]{2,0,1:T(2,128)S(1)} fusion(f32[2,128,4,1792]{3,0,2,1:T(2,128)} %copy.17, f32[2,512,1792]{2,1,0:T(8,128)} %param.4), kind=kLoop, calls=%fused_computation | loop fusion | flops 1835008 | bytes 22020096 | tf_op jit(solution)/shard_map/sub | solution.py:28
  264.3 3.6 %copy.19 = f32[2,512,1792]{2,1,0:T(8,128)} copy(f32[2,512,1792]{2,0,1:T(2,128)S(1)} %bitcast_subtract_fusion) | data formatting | bytes 14680064
Async XLA Ops:
  7.2 234.2 %all-gather.2.cloned.1.call-start = ((), (), s32[]{:S(2)}) async-start(), calls=%async_computation.2 | async-start | bytes 9175040 | tf_op jit(solution)/shard_map/all_gather | solution.py:27
  135.6 1.5 copy-start
Sparse Core Ops, SparseCore 0:
  171.2 70.0 all-gather.1
where the time goes:
time: 275 us
  blocking collectives  129 us (47%)
  waiting for transfers between devices  70.3 us (26%)
  local copies, waits for them, and re-layouts  31.4 us (11%)
  other arithmetic  29.7 us (11%)
  between operations  14.1 us (5%)
    all_to_all x1, blocking collectives, body(): lax.all_to_all(pieces, ('grp', 'shard', 'tp'), split_axis=1, concat_axis=...  97.7 us
    all_gather x1, waiting for transfers between devices, body(): gathered = lax.all_gather(own_part, 'grp', axis=1, tiled=True)  70.2 us
    all_to_all x1, blocking collectives, body(): lax.all_to_all(outgoing, ('shard', 'tp'), split_axis=1, concat_axis=1, ti...  31.6 us
    sub x1, other arithmetic, body(): new_weights = start_weights - gathered.reshape(2, row_count, col_count)  13.1 us
    sub x1, local copies, waits for them, and re-layouts, body(): differ = start_weights - inner_weights[0]  11.7 us
    all_gather x1, local copies, waits for them, and re-layouts, body(): gathered = lax.all_gather(own_part, 'grp', axis=1, tiled=True)  9.9 us
    sub x1, other arithmetic, body(): differ = start_weights - inner_weights[0]  9.12 us
  transfers between devices with their start and end apart: 1, of which 1 were waited for; matrix products, arithmetic and copies ran while one was open for 0% of the time, Pallas kernels for 0%

commit v1 on v0

v1 whole, which is shorter than its diff:
```python
import functools

import jax
import jax.numpy as jnp
from jax import lax
from jax.experimental import pallas as pl
from jax.experimental.pallas import tpu as pltpu
from jax.sharding import PartitionSpec as P

OUTER_RATE = 0.7
MOMENTUM_COEF = 0.5
CHUNKS = 4
UP, DOWN = 0, 1
FAR, NEAR, RELAY, OUT_FAR, OUT_NEAR, OUT_RELAY = range(6)
MESH = pl.DeviceIdType.MESH


def kernel(
    inner, start, mom, new_w, new_mom,
    diff, base, land, mom_in, mom_out, own_w,
    load_sem, z_send, z_recv, in_send, in_recv, out_send, out_recv, local_sem,
):
    groups, shards, tps = lax.axis_size("grp"), lax.axis_size("shard"), lax.axis_size("tp")
    plane = shards * tps
    g, s, t = lax.axis_index("grp"), lax.axis_index("shard"), lax.axis_index("tp")
    me = s * tps + t
    up, down, far = (g + 1) % groups, (g + groups - 1) % groups, (g + 2) % groups
    rows = start.shape[1] // groups
    step = rows // CHUNKS
    q_rows = mom.shape[2]
    per_step = step // q_rows
    side = ((up, s, t), (down, s, t))

    def at_rows(quarter, c):
        return pl.ds(pl.multiple_of(quarter * rows + c * step, step), step)

    def in_chunk(c):
        return pl.ds(pl.multiple_of(c * step, step), step)

    def load(slot, a, quarter, begin):
        where = pl.ds(pl.multiple_of(quarter * rows, rows), rows)
        for k, (src, dst) in enumerate(((inner, diff), (start, base))):
            copy = pltpu.make_async_copy(src.at[a, where], dst.at[a, where], load_sem.at[slot, k])
            copy.start() if begin else copy.wait()

    blocks = ((0, far), (1, far), (1, up), (0, down), (0, up), (1, down), (0, g), (1, g))

    def subtract(a, quarter):
        def one(c, carry):
            where = at_rows(quarter, c)
            diff[a, where] = base[a, where] - diff[a, where]
            return carry
        lax.fori_loop(0, CHUNKS, one, 0)

    def z_copy(direction, kind, c, src, dst):
        return pltpu.make_async_remote_copy(
            src_ref=src, dst_ref=dst,
            send_sem=z_send.at[direction, kind, c], recv_sem=z_recv.at[direction, kind, c],
            device_id=side[direction], device_id_type=MESH)

    def sum_copy(direction, kind, c, quarter, a):
        slot = land.at[direction, kind, in_chunk(c)]
        return z_copy(direction, kind, c, diff.at[a, at_rows(quarter, c)], slot)

    def own_copy(direction, kind, c, a):
        return z_copy(direction, kind, c, own_w.at[a, in_chunk(c)], new_w.at[a, at_rows(g, c)])

    def relay_copy(direction, c, quarter, a):
        where = at_rows(quarter, c)
        return z_copy(direction, OUT_RELAY, c, new_w.at[a, where], new_w.at[a, where])

    def partner(k):
        other = (me + k) % plane
        return other, (g, other // tps, other % tps)

    def in_copy(k):
        other, device = partner(k)
        return pltpu.make_async_remote_copy(
            src_ref=mom.at[:, other], dst_ref=mom_in.at[:, me],
            send_sem=in_send.at[other], recv_sem=in_recv.at[me],
            device_id=device, device_id_type=MESH)

    def in_arrival(other):
        return pltpu.make_async_copy(mom_in.at[:, other], mom_in.at[:, other], in_recv.at[other])

    def out_copy(other):
        return pltpu.make_async_remote_copy(
            src_ref=mom_out.at[:, other], dst_ref=new_mom.at[:, me],
            send_sem=out_send.at[other], recv_sem=out_recv.at[me],
            device_id=(g, other // tps, other % tps), device_id_type=MESH)

    def out_arrival(other):
        return pltpu.make_async_copy(new_mom.at[:, other], new_mom.at[:, other], out_recv.at[other])

    def loop(n, body):
        def one(i, carry):
            body(i)
            return carry
        lax.fori_loop(0, n, one, 0)

    for slot in (0, 1):
        load(slot, *blocks[slot], True)

    barrier = pltpu.get_barrier_semaphore()
    for device in side:
        pl.semaphore_signal(barrier, inc=1, device_id=device, device_id_type=MESH)

    def greet(k):
        pl.semaphore_signal(barrier, inc=1, device_id=partner(k + 1)[1], device_id_type=MESH)
    loop(plane - 1, greet)
    pl.semaphore_wait(barrier, plane + 1)

    for slot in (0, 1):
        load(slot, *blocks[slot], False)

    def send_far(c):
        for a in (0, 1):
            where = at_rows(far, c)
            diff[a, where] = base[a, where] - diff[a, where]
        sum_copy(UP, FAR, c, far, 0).start()
        sum_copy(DOWN, FAR, c, far, 1).start()
    loop(CHUNKS, send_far)

    for slot in range(2, 8):
        load(slot, *blocks[slot], True)
    own_in = pltpu.make_async_copy(mom.at[:, me], mom_in.at[:, me], local_sem.at[0])
    own_in.start()
    loop(plane - 1, lambda k: in_copy(k + 1).start())

    for slot in (2, 3):
        load(slot, *blocks[slot], False)

    def send_near(c):
        for a, quarter in ((1, up), (0, down)):
            where = at_rows(quarter, c)
            diff[a, where] = base[a, where] - diff[a, where]
        sum_copy(UP, NEAR, c, up, 1).start()
        sum_copy(DOWN, NEAR, c, down, 0).start()
    loop(CHUNKS, send_near)

    for slot in range(4, 8):
        load(slot, *blocks[slot], False)
        subtract(*blocks[slot])

    def send_relay(c):
        for direction, a, quarter in ((UP, 0, up), (DOWN, 1, down)):
            sum_copy(direction, FAR, c, far, a).wait_recv()
            where = at_rows(quarter, c)
            diff[a, where] = diff[a, where] + land[direction, FAR, in_chunk(c)]
        sum_copy(UP, RELAY, c, up, 0).start()
        sum_copy(DOWN, RELAY, c, down, 1).start()
    loop(CHUNKS, send_relay)

    own_in.wait()
    loop(plane - 1, lambda k: in_arrival((me + k + 1) % plane).wait())

    def finish(c):
        for direction, near_a, relay_a in ((UP, 1, 0), (DOWN, 0, 1)):
            sum_copy(direction, NEAR, c, up, near_a).wait_recv()
            sum_copy(direction, RELAY, c, up, relay_a).wait_recv()

        def pair(i):
            for a, near, relay in ((0, DOWN, UP), (1, UP, DOWN)):
                local = pl.ds(pl.multiple_of(c * step + i * 2 * q_rows, 2 * q_rows), 2 * q_rows)
                where = pl.ds(pl.multiple_of(g * rows + c * step + i * 2 * q_rows, 2 * q_rows), 2 * q_rows)
                j = c * per_step + 2 * i
                total = diff[a, where] + land[near, NEAR, local] + land[relay, RELAY, local]
                flat = total / groups
                old = jnp.concatenate([mom_in[a, j], mom_in[a, j + 1]], axis=0)
                fresh = MOMENTUM_COEF * old + flat
                mom_out[a, j] = fresh[:q_rows]
                mom_out[a, j + 1] = fresh[q_rows:]
                own_w[a, local] = base[a, where] - OUTER_RATE * (flat + MOMENTUM_COEF * fresh)
        loop(per_step // 2, pair)
        own_copy(UP, OUT_FAR, c, 0).start()
        own_copy(DOWN, OUT_FAR, c, 1).start()
        own_copy(UP, OUT_NEAR, c, 1).start()
        own_copy(DOWN, OUT_NEAR, c, 0).start()

        def give(i):
            other = c * per_step + i

            @pl.when(other != me)
            def _():
                out_copy(other).start()
        loop(per_step, give)
    loop(CHUNKS, finish)
    mine = pl.ds(pl.multiple_of(g * rows, rows), rows)
    keep_w = pltpu.make_async_copy(own_w, new_w.at[:, mine], local_sem.at[1])
    keep_mom = pltpu.make_async_copy(mom_out.at[:, me], new_mom.at[:, me], local_sem.at[2])
    keep_w.start()
    keep_mom.start()

    def pass_on(c):
        for direction, source, a in ((UP, down, 0), (DOWN, up, 1)):
            own_copy(direction, OUT_FAR, c, a).wait_recv()
            relay_copy(direction, c, source, a).start()
    loop(CHUNKS, pass_on)

    def drain(c):
        for direction, near_a, a in ((UP, 1, 0), (DOWN, 0, 1)):
            own_copy(direction, OUT_NEAR, c, near_a).wait_recv()
            relay_copy(direction, c, far, a).wait_recv()
        for direction in (UP, DOWN):
            for kind in (FAR, NEAR, RELAY, OUT_FAR, OUT_NEAR, OUT_RELAY):
                z_copy(direction, kind, c, own_w.at[0, in_chunk(c)], own_w.at[0, in_chunk(c)]).wait_send()
    loop(CHUNKS, drain)
    keep_w.wait()
    keep_mom.wait()

    def drain_plane(k):
        other = (me + k + 1) % plane
        in_copy(k + 1).wait_send()
        out_copy(other).wait_send()
        out_arrival(other).wait()
    loop(plane - 1, drain_plane)


def body(inner_weights, start_weights, momentum):
    groups, shards, tps = lax.axis_size("grp"), lax.axis_size("shard"), lax.axis_size("tp")
    plane = shards * tps
    mats, row_count, col_count = start_weights.shape
    q_rows = momentum.shape[4]
    quarter = row_count // groups
    any_spec = pl.BlockSpec(memory_space=pl.ANY)
    flat_shape = (mats, plane, q_rows, col_count)
    dma = pltpu.SemaphoreType.DMA
    new_w, new_mom = pl.pallas_call(
        kernel,
        out_shape=(
            jax.ShapeDtypeStruct(start_weights.shape, jnp.float32),
            jax.ShapeDtypeStruct(flat_shape, jnp.float32),
        ),
        in_specs=[any_spec] * 3,
        out_specs=(any_spec, any_spec),
        scratch_shapes=[
            pltpu.VMEM(start_weights.shape, jnp.float32),
            pltpu.VMEM(start_weights.shape, jnp.float32),
            pltpu.VMEM((2, 3, quarter, col_count), jnp.float32),
            pltpu.VMEM(flat_shape, jnp.float32),
            pltpu.VMEM(flat_shape, jnp.float32),
            pltpu.VMEM((mats, quarter, col_count), jnp.float32),
            dma((8, 2)),
            dma((2, 6, CHUNKS)),
            dma((2, 6, CHUNKS)),
            dma((plane,)),
            dma((plane,)),
            dma((plane,)),
            dma((plane,)),
            dma((3,)),
        ],
        compiler_params=pltpu.CompilerParams(collective_id=0, has_side_effects=True, vmem_limit_bytes=60000000),
        name="outer_step",
    )(inner_weights[0], start_weights, momentum.reshape(flat_shape))
    return new_w, new_mom.reshape(momentum.shape)


def solution(mesh):
    in_specs = (
        P("grp", None, "shard", "tp"),
        P(None, "shard", "tp"),
        P(None, None, None, ("grp", "shard", "tp"), None, None),
    )
    out_specs = (P(None, "shard", "tp"), P(None, None, None, ("grp", "shard", "tp"), None, None))
    return jax.shard_map(body, mesh=mesh, in_specs=in_specs, out_specs=out_specs, check_vma=False)
```

time: 275 us -> 141 us (0.51)
  Pallas kernels: 0 us -> 132 us
  blocking collectives: 129 us -> 0 us
  waiting for transfers between devices: 70.3 us -> 0 us
  other arithmetic: 29.7 us -> 0 us
  local copies, waits for them, and re-layouts: 31.4 us -> 7.97 us
  between operations: 14.1 us -> 0.65 us
    pallas_call x0 -> x1, Pallas kernels: none -> 132 us  [body(): pl.pallas_call(kernel, out_shape=(jax.ShapeDtypeStruct(start_weights.shap...]
    all_to_all x2 -> x0, blocking collectives: 129 us -> none  [the longest x1 97.7 us: body(): lax.all_to_all(pieces, ('grp', 'shard', 'tp'), split_axis=1, concat_axis=...]
    all_gather x1 -> x0, waiting for transfers between devices: 70.2 us -> none  [body(): gathered = lax.all_gather(own_part, 'grp', axis=1, tiled=True)]
    sub x2 -> x0, other arithmetic: 22.2 us -> none  [the longest x1 13.1 us: body(): new_weights = start_weights - gathered.reshape(2, row_count, col_count)]
    sub x1 -> x0, local copies, waits for them, and re-layouts: 11.7 us -> none  [body(): differ = start_weights - inner_weights[0]]
    all_gather x1 -> x0, local copies, waits for them, and re-layouts: 9.9 us -> none  [body(): gathered = lax.all_gather(own_part, 'grp', axis=1, tiled=True)]
    reshape x1 -> x0, local copies, waits for them, and re-layouts: 4.97 us -> none  [body(): pieces = differ.reshape(2, devices, q_rows, col_count)]
    reduce_sum x1 -> x0, other arithmetic: 4.89 us -> none  [body(): jnp.sum(landed.reshape(2, groups, shards * tp_size, q_rows, col_count), a...]
  transfers between devices with their start and end apart: 1 -> 0, of which waited for: 1 -> 0; matrix products, arithmetic and copies ran while one was open for 0% -> 0% of each run, Pallas kernels for 0% -> 0%
where the time goes in v1:
time: 141 us
  Pallas kernels  132 us (94%)
  local copies, waits for them, and re-layouts  7.97 us (6%)
    pallas_call x1, Pallas kernels, body(): pl.pallas_call(kernel, out_shape=(jax.ShapeDtypeStruct(start_weights.shap...  132 us
    unnamed x4, local copies, waits for them, and re-layouts  7.97 us

profile of v1, /device:TPU:1, one launch (start us, length us, event | category | flops | bytes accessed | tf_op | source)
XLA Modules:
  0.0 141.0 jit_solution(7270134957757179974)
XLA Ops:
  0.6 132.4 %outer_step.1 = (f32[2,512,1792]{2,1,0:T(8,128)}, f32[2,32,4,1792]{3,2,1,0:T(4,128)}) custom-call(f32[2,512,1792]{2,1,0:T(8,128)} %bitcast.5, f32[2,512,1792]{2,1,0:T(8,128)} %start.1, f32[2,32,4,1792]{3,2,1,0:T(4,128)} %bitcast.7), custom_call_target="tpu_custom_call" | custom-call | tf_op jit(solution)/shard_map/outer_step/pallas_call | solution.py:228
  133.0 0.0 copy-start
  133.0 6.7 %copy.8 = f32[2,512,1792]{2,1,0:T(8,128)} copy(f32[2,512,1792]{2,1,0:T(8,128)} %get-tuple-element.10) | data formatting | bytes 14680064
  139.8 0.0 copy-done
  139.8 1.2 copy.9
Async XLA Ops:
  133.0 6.7 %copy-start = (f32[2,32,4,1792]{3,2,1,0:T(4,128)S(1)}, f32[2,32,4,1792]{3,2,1,0:T(4,128)}, u32[]{:S(2)}) copy-start(f32[2,32,4,1792]{3,2,1,0:T(4,128)} %get-tuple-element.5) | copy-start | bytes 5505028

commit v2 on v1

--- a/solution.py
+++ b/solution.py
@@ -17,8 +17,8 @@
 
 def kernel(
     inner, start, mom, new_w, new_mom,
-    diff, base, land, mom_in, mom_out, own_w,
-    load_sem, z_send, z_recv, in_send, in_recv, out_send, out_recv, local_sem,
+    diff, base, land, mom_in, mom_out,
+    load_sem, z_send, z_recv, in_send, in_recv, out_send, out_recv, local_sem, word_sem,
 ):
     groups, shards, tps = lax.axis_size("grp"), lax.axis_size("shard"), lax.axis_size("tp")
     plane = shards * tps
@@ -63,7 +63,8 @@
         return z_copy(direction, kind, c, diff.at[a, at_rows(quarter, c)], slot)
 
     def own_copy(direction, kind, c, a):
-        return z_copy(direction, kind, c, own_w.at[a, in_chunk(c)], new_w.at[a, at_rows(g, c)])
+        where = at_rows(g, c)
+        return z_copy(direction, kind, c, new_w.at[a, where], new_w.at[a, where])
 
     def relay_copy(direction, c, quarter, a):
         where = at_rows(quarter, c)
@@ -101,14 +102,31 @@
     for slot in (0, 1):
         load(slot, *blocks[slot], True)
 
+    x_size, y_low = shards // 2, tps // 2
+    x, y, core = s % x_size, (s // x_size) * y_low + t // 2, t % 2
+
+    def seat(dx, dy, dcore):
+        nx, ny = (x + dx + x_size) % x_size, (y + dy + 2 * y_low) % (2 * y_low)
+        return (g, (ny // y_low) * x_size + nx, (ny % y_low) * 2 + (core + dcore) % 2)
+
+    along_x, along_y, beside = (seat(1, 0, 0), seat(-1, 0, 0)), (seat(0, 1, 0), seat(0, -1, 0)), (seat(0, 0, 1),)
+
     barrier = pltpu.get_barrier_semaphore()
-    for device in side:
+    nearest = side + along_x + along_y + beside
+    for device in nearest:
         pl.semaphore_signal(barrier, inc=1, device_id=device, device_id_type=MESH)
-
-    def greet(k):
-        pl.semaphore_signal(barrier, inc=1, device_id=partner(k + 1)[1], device_id_type=MESH)
-    loop(plane - 1, greet)
-    pl.semaphore_wait(barrier, plane + 1)
+    pl.semaphore_wait(barrier, len(nearest))
+
+    rounds = (along_x, along_y, along_x, beside)
+
+    def tell(i):
+        for device in rounds[i]:
+            pl.semaphore_signal(word_sem.at[i], inc=1, device_id=device, device_id_type=MESH)
+
+    def hear(i):
+        pl.semaphore_wait(word_sem.at[i], len(rounds[i]))
+
+    tell(0)
 
     for slot in (0, 1):
         load(slot, *blocks[slot], False)
@@ -125,7 +143,8 @@
         load(slot, *blocks[slot], True)
     own_in = pltpu.make_async_copy(mom.at[:, me], mom_in.at[:, me], local_sem.at[0])
     own_in.start()
-    loop(plane - 1, lambda k: in_copy(k + 1).start())
+    hear(0)
+    tell(1)
 
     for slot in (2, 3):
         load(slot, *blocks[slot], False)
@@ -138,9 +157,18 @@
         sum_copy(DOWN, NEAR, c, down, 0).start()
     loop(CHUNKS, send_near)
 
-    for slot in range(4, 8):
+    hear(1)
+    tell(2)
+    for slot in (4, 5):
         load(slot, *blocks[slot], False)
         subtract(*blocks[slot])
+    hear(2)
+    tell(3)
+    for slot in (6, 7):
+        load(slot, *blocks[slot], False)
+        subtract(*blocks[slot])
+    hear(3)
+    loop(plane - 1, lambda k: in_copy(k + 1).start())
 
     def send_relay(c):
         for direction, a, quarter in ((UP, 0, up), (DOWN, 1, down)):
@@ -170,7 +198,7 @@
                 fresh = MOMENTUM_COEF * old + flat
                 mom_out[a, j] = fresh[:q_rows]
                 mom_out[a, j + 1] = fresh[q_rows:]
-                own_w[a, local] = base[a, where] - OUTER_RATE * (flat + MOMENTUM_COEF * fresh)
+                new_w[a, where] = base[a, where] - OUTER_RATE * (flat + MOMENTUM_COEF * fresh)
         loop(per_step // 2, pair)
         own_copy(UP, OUT_FAR, c, 0).start()
         own_copy(DOWN, OUT_FAR, c, 1).start()
@@ -185,11 +213,7 @@
                 out_copy(other).start()
         loop(per_step, give)
     loop(CHUNKS, finish)
-    mine = pl.ds(pl.multiple_of(g * rows, rows), rows)
-    keep_w = pltpu.make_async_copy(own_w, new_w.at[:, mine], local_sem.at[1])
-    keep_mom = pltpu.make_async_copy(mom_out.at[:, me], new_mom.at[:, me], local_sem.at[2])
-    keep_w.start()
-    keep_mom.start()
+    new_mom[:, me] = mom_out[:, me]
 
     def pass_on(c):
         for direction, source, a in ((UP, down, 0), (DOWN, up, 1)):
@@ -203,10 +227,8 @@
             relay_copy(direction, c, far, a).wait_recv()
         for direction in (UP, DOWN):
             for kind in (FAR, NEAR, RELAY, OUT_FAR, OUT_NEAR, OUT_RELAY):
-                z_copy(direction, kind, c, own_w.at[0, in_chunk(c)], own_w.at[0, in_chunk(c)]).wait_send()
+                own_copy(direction, kind, c, 0).wait_send()
     loop(CHUNKS, drain)
-    keep_w.wait()
-    keep_mom.wait()
 
     def drain_plane(k):
         other = (me + k + 1) % plane
@@ -228,18 +250,17 @@
     new_w, new_mom = pl.pallas_call(
         kernel,
         out_shape=(
-            jax.ShapeDtypeStruct(start_weights.shape, jnp.float32),
-            jax.ShapeDtypeStruct(flat_shape, jnp.float32),
+            pltpu.VMEM(start_weights.shape, jnp.float32),
+            pltpu.VMEM(flat_shape, jnp.float32),
         ),
         in_specs=[any_spec] * 3,
-        out_specs=(any_spec, any_spec),
+        out_specs=(pl.BlockSpec(memory_space=pltpu.VMEM),) * 2,
         scratch_shapes=[
             pltpu.VMEM(start_weights.shape, jnp.float32),
             pltpu.VMEM(start_weights.shape, jnp.float32),
             pltpu.VMEM((2, 3, quarter, col_count), jnp.float32),
             pltpu.VMEM(flat_shape, jnp.float32),
             pltpu.VMEM(flat_shape, jnp.float32),
-            pltpu.VMEM((mats, quarter, col_count), jnp.float32),
             dma((8, 2)),
             dma((2, 6, CHUNKS)),
             dma((2, 6, CHUNKS)),
@@ -247,9 +268,10 @@
             dma((plane,)),
             dma((plane,)),
             dma((plane,)),
-            dma((3,)),
+            dma((1,)),
+            pltpu.SemaphoreType.REGULAR((4,)),
         ],
-        compiler_params=pltpu.CompilerParams(collective_id=0, has_side_effects=True, vmem_limit_bytes=60000000),
+        compiler_params=pltpu.CompilerParams(collective_id=0, has_side_effects=True, vmem_limit_bytes=50000000),
         name="outer_step",
     )(inner_weights[0], start_weights, momentum.reshape(flat_shape))
     return new_w, new_mom.reshape(momentum.shape)

time: 141 us -> 134 us (0.950)
  Pallas kernels: 132 us -> 128 us
  local copies, waits for them, and re-layouts: 7.97 us -> 4.28 us
    pallas_call x1, Pallas kernels: 132 us -> 128 us  [body(): pl.pallas_call(kernel, out_shape=(pltpu.VMEM(start_weights.shape, jnp.flo...]
    unnamed x4 -> x2, local copies, waits for them, and re-layouts: 7.97 us -> 4.28 us
where the time goes in v2:
time: 134 us; the launch traced here: 133 us
  Pallas kernels  128 us (96%)
  local copies, waits for them, and re-layouts  4.28 us (3%)
    pallas_call x1, Pallas kernels, body(): pl.pallas_call(kernel, out_shape=(pltpu.VMEM(start_weights.shape, jnp.flo...  128 us
    unnamed x2, local copies, waits for them, and re-layouts  4.28 us

profile of v2, /device:TPU:1, one launch (start us, length us, event | category | flops | bytes accessed | tf_op | source)
XLA Modules:
  0.0 133.3 jit_solution(780154661053298296)
XLA Ops:
  0.6 128.4 %outer_step.1 = (f32[2,512,1792]{2,1,0:T(8,128)S(1)}, f32[2,32,4,1792]{3,2,1,0:T(4,128)S(1)}) custom-call(f32[2,512,1792]{2,1,0:T(8,128)} %bitcast.6, f32[2,512,1792]{2,1,0:T(8,128)} %start.1, f32[2,32,4,1792]{3,2,1,0:T(4,128)} %bitcast.7), custom_call_target="tpu_custom_call" | custom-call | tf_op jit(solution)/shard_map/outer_step/pallas_call | solution.py:250
  129.0 3.1 %copy.8 = f32[2,512,1792]{2,1,0:T(8,128)} copy(f32[2,512,1792]{2,1,0:T(8,128)S(1)} %get-tuple-element.8) | data formatting | bytes 14680064
  132.1 1.2 copy.9

commit v3 on v2

--- a/solution.py
+++ b/solution.py
@@ -9,7 +9,7 @@
 
 OUTER_RATE = 0.7
 MOMENTUM_COEF = 0.5
-CHUNKS = 4
+CHUNKS = 2
 UP, DOWN = 0, 1
 FAR, NEAR, RELAY, OUT_FAR, OUT_NEAR, OUT_RELAY = range(6)
 MESH = pl.DeviceIdType.MESH
@@ -18,7 +18,7 @@
 def kernel(
     inner, start, mom, new_w, new_mom,
     diff, base, land, mom_in, mom_out,
-    load_sem, z_send, z_recv, in_send, in_recv, out_send, out_recv, local_sem, word_sem,
+    load_sem, z_send, z_recv, in_send, in_recv, out_send, out_recv, local_sem, near_sem, word_sem,
 ):
     groups, shards, tps = lax.axis_size("grp"), lax.axis_size("shard"), lax.axis_size("tp")
     plane = shards * tps
@@ -43,7 +43,7 @@
             copy = pltpu.make_async_copy(src.at[a, where], dst.at[a, where], load_sem.at[slot, k])
             copy.start() if begin else copy.wait()
 
-    blocks = ((0, far), (1, far), (1, up), (0, down), (0, up), (1, down), (0, g), (1, g))
+    blocks = ((0, up), (1, down), (0, g), (1, g))
 
     def subtract(a, quarter):
         def one(c, carry):
@@ -59,8 +59,9 @@
             device_id=side[direction], device_id_type=MESH)
 
     def sum_copy(direction, kind, c, quarter, a):
+        source = diff if kind == RELAY else inner
         slot = land.at[direction, kind, in_chunk(c)]
-        return z_copy(direction, kind, c, diff.at[a, at_rows(quarter, c)], slot)
+        return z_copy(direction, kind, c, source.at[a, at_rows(quarter, c)], slot)
 
     def own_copy(direction, kind, c, a):
         where = at_rows(g, c)
@@ -99,9 +100,6 @@
             return carry
         lax.fori_loop(0, n, one, 0)
 
-    for slot in (0, 1):
-        load(slot, *blocks[slot], True)
-
     x_size, y_low = shards // 2, tps // 2
     x, y, core = s % x_size, (s // x_size) * y_low + t // 2, t % 2
 
@@ -111,70 +109,91 @@
 
     along_x, along_y, beside = (seat(1, 0, 0), seat(-1, 0, 0)), (seat(0, 1, 0), seat(0, -1, 0)), (seat(0, 0, 1),)
 
+    def signal(sem, *devices):
+        for device in devices:
+            pl.semaphore_signal(sem, inc=1, device_id=device, device_id_type=MESH)
+
     barrier = pltpu.get_barrier_semaphore()
-    nearest = side + along_x + along_y + beside
-    for device in nearest:
-        pl.semaphore_signal(barrier, inc=1, device_id=device, device_id_type=MESH)
-    pl.semaphore_wait(barrier, len(nearest))
-
-    rounds = (along_x, along_y, along_x, beside)
-
-    def tell(i):
-        for device in rounds[i]:
-            pl.semaphore_signal(word_sem.at[i], inc=1, device_id=device, device_id_type=MESH)
+
+    @pl.when(g == 0)
+    def _():
+        signal(barrier, *side, *along_x, *along_y, *beside)
+
+    @pl.when(g == 1)
+    def _():
+        signal(barrier, side[UP])
+
+    @pl.when(g == 3)
+    def _():
+        signal(barrier, side[DOWN])
+    pl.semaphore_wait(barrier, jnp.where(g == 0, 5, jnp.where(g == 2, 2, 1)))
+
+    @pl.when((g == 1) | (g == 2))
+    def _():
+        signal(near_sem.at[UP], side[DOWN])
+
+    @pl.when((g == 3) | (g == 2))
+    def _():
+        signal(near_sem.at[DOWN], side[UP])
+
+    def send_raw(direction, a, owner):
+        loop(CHUNKS, lambda c: sum_copy(direction, FAR, c, far, a).start())
+        loop(CHUNKS, lambda c: sum_copy(direction, NEAR, c, owner, 1 - a).start())
+
+    @pl.when(g == 1)
+    def _():
+        send_raw(DOWN, 1, down)
+
+    @pl.when(g < 2)
+    def _():
+        pl.semaphore_wait(near_sem.at[UP], 1)
+    send_raw(UP, 0, up)
+
+    @pl.when((g == 0) | (g == 3))
+    def _():
+        pl.semaphore_wait(near_sem.at[DOWN], 1)
+
+    @pl.when(g != 1)
+    def _():
+        send_raw(DOWN, 1, down)
+
+    @pl.when(g == 1)
+    def _():
+        signal(word_sem.at[0], side[DOWN])
+
+    rounds = (along_x, along_y, along_x, along_y, beside)
 
     def hear(i):
-        pl.semaphore_wait(word_sem.at[i], len(rounds[i]))
-
-    tell(0)
-
-    for slot in (0, 1):
-        load(slot, *blocks[slot], False)
-
-    def send_far(c):
-        for a in (0, 1):
-            where = at_rows(far, c)
-            diff[a, where] = base[a, where] - diff[a, where]
-        sum_copy(UP, FAR, c, far, 0).start()
-        sum_copy(DOWN, FAR, c, far, 1).start()
-    loop(CHUNKS, send_far)
-
-    for slot in range(2, 8):
+        @pl.when(g == 0)
+        def _():
+            pl.semaphore_wait(word_sem.at[i], 1 if i == 0 else len(rounds[i - 1]))
+            if i < len(rounds):
+                signal(word_sem.at[i + 1], *rounds[i])
+            else:
+                signal(word_sem.at[i + 1], (up, s, t), (far, s, t), (down, s, t))
+
+    for slot in range(4):
         load(slot, *blocks[slot], True)
     own_in = pltpu.make_async_copy(mom.at[:, me], mom_in.at[:, me], local_sem.at[0])
     own_in.start()
+
     hear(0)
-    tell(1)
-
-    for slot in (2, 3):
-        load(slot, *blocks[slot], False)
-
-    def send_near(c):
-        for a, quarter in ((1, up), (0, down)):
-            where = at_rows(quarter, c)
-            diff[a, where] = base[a, where] - diff[a, where]
-        sum_copy(UP, NEAR, c, up, 1).start()
-        sum_copy(DOWN, NEAR, c, down, 0).start()
-    loop(CHUNKS, send_near)
-
-    hear(1)
-    tell(2)
-    for slot in (4, 5):
+    for slot in range(4):
         load(slot, *blocks[slot], False)
         subtract(*blocks[slot])
-    hear(2)
-    tell(3)
-    for slot in (6, 7):
-        load(slot, *blocks[slot], False)
-        subtract(*blocks[slot])
-    hear(3)
+        hear(slot + 1)
+    hear(5)
+
+    @pl.when(g != 0)
+    def _():
+        pl.semaphore_wait(word_sem.at[6], 1)
     loop(plane - 1, lambda k: in_copy(k + 1).start())
 
     def send_relay(c):
         for direction, a, quarter in ((UP, 0, up), (DOWN, 1, down)):
             sum_copy(direction, FAR, c, far, a).wait_recv()
             where = at_rows(quarter, c)
-            diff[a, where] = diff[a, where] + land[direction, FAR, in_chunk(c)]
+            diff[a, where] = diff[a, where] + (base[a, where] - land[direction, FAR, in_chunk(c)])
         sum_copy(UP, RELAY, c, up, 0).start()
         sum_copy(DOWN, RELAY, c, down, 1).start()
     loop(CHUNKS, send_relay)
@@ -192,7 +211,7 @@
                 local = pl.ds(pl.multiple_of(c * step + i * 2 * q_rows, 2 * q_rows), 2 * q_rows)
                 where = pl.ds(pl.multiple_of(g * rows + c * step + i * 2 * q_rows, 2 * q_rows), 2 * q_rows)
                 j = c * per_step + 2 * i
-                total = diff[a, where] + land[near, NEAR, local] + land[relay, RELAY, local]
+                total = diff[a, where] + (base[a, where] - land[near, NEAR, local]) + land[relay, RELAY, local]
                 flat = total / groups
                 old = jnp.concatenate([mom_in[a, j], mom_in[a, j + 1]], axis=0)
                 fresh = MOMENTUM_COEF * old + flat
@@ -236,6 +255,20 @@
         out_copy(other).wait_send()
         out_arrival(other).wait()
     loop(plane - 1, drain_plane)
+
+
+def write_out(new_w, new_mom, out_w, out_mom, sem):
+    copies = []
+    for a in range(new_w.shape[0]):
+        half = new_w.shape[1] // 2
+        for part in range(2):
+            where = (a, pl.ds(part * half, half))
+            copies.append(pltpu.make_async_copy(new_w.at[where], out_w.at[where], sem.at[len(copies)]))
+        copies.append(pltpu.make_async_copy(new_mom.at[a], out_mom.at[a], sem.at[len(copies)]))
+    for copy in copies:
+        copy.start()
+    for copy in copies:
+        copy.wait()
 
 
 def body(inner_weights, start_weights, momentum):
@@ -261,7 +294,7 @@
             pltpu.VMEM((2, 3, quarter, col_count), jnp.float32),
             pltpu.VMEM(flat_shape, jnp.float32),
             pltpu.VMEM(flat_shape, jnp.float32),
-            dma((8, 2)),
+            dma((4, 2)),
             dma((2, 6, CHUNKS)),
             dma((2, 6, CHUNKS)),
             dma((plane,)),
@@ -269,12 +302,26 @@
             dma((plane,)),
             dma((plane,)),
             dma((1,)),
-            pltpu.SemaphoreType.REGULAR((4,)),
+            pltpu.SemaphoreType.REGULAR((2,)),
+            pltpu.SemaphoreType.REGULAR((7,)),
         ],
         compiler_params=pltpu.CompilerParams(collective_id=0, has_side_effects=True, vmem_limit_bytes=50000000),
         name="outer_step",
     )(inner_weights[0], start_weights, momentum.reshape(flat_shape))
-    return new_w, new_mom.reshape(momentum.shape)
+    vmem_spec = pl.BlockSpec(memory_space=pltpu.VMEM)
+    out_w, out_mom = pl.pallas_call(
+        write_out,
+        out_shape=(
+            jax.ShapeDtypeStruct(start_weights.shape, jnp.float32),
+            jax.ShapeDtypeStruct(flat_shape, jnp.float32),
+        ),
+        in_specs=[vmem_spec] * 2,
+        out_specs=(any_spec, any_spec),
+        scratch_shapes=[dma((6,))],
+        compiler_params=pltpu.CompilerParams(vmem_limit_bytes=4000000),
+        name="write_out",
+    )(new_w, new_mom)
+    return out_w, out_mom.reshape(momentum.shape)
 
 
 def solution(mesh):

time: 134 us -> 130 us (0.970)
  local copies, waits for them, and re-layouts: 4.28 us -> 0 us
    unnamed x2 -> x0, local copies, waits for them, and re-layouts: 4.28 us -> none
    pallas_call x0 -> x1, Pallas kernels: none -> 3.59 us  [body(): pl.pallas_call(write_out, out_shape=(jax.ShapeDtypeStruct(start_weights.s...]
    pallas_call x1, Pallas kernels: 128 us -> 126 us  [body(): pl.pallas_call(kernel, out_shape=(pltpu.VMEM(start_weights.shape, jnp.flo...]
where the time goes in v3:
time: 130 us
  Pallas kernels  129 us (99%)
    pallas_call x1, Pallas kernels, body(): pl.pallas_call(kernel, out_shape=(pltpu.VMEM(start_weights.shape, jnp.flo...  126 us
    pallas_call x1, Pallas kernels, body(): pl.pallas_call(write_out, out_shape=(jax.ShapeDtypeStruct(start_weights.s...  3.59 us

profile of v3, /device:TPU:1, one launch (start us, length us, event | category | flops | bytes accessed | tf_op | source)
XLA Modules:
  0.0 129.9 jit_solution(5156553329991034359)
XLA Ops:
  0.6 125.7 %outer_step.1 = (f32[2,512,1792]{2,1,0:T(8,128)S(1)}, f32[2,32,4,1792]{3,2,1,0:T(4,128)S(1)}) custom-call(f32[2,512,1792]{2,1,0:T(8,128)} %bitcast.5, f32[2,512,1792]{2,1,0:T(8,128)} %start.1, f32[2,32,4,1792]{3,2,1,0:T(4,128)} %bitcast.6), custom_call_target="tpu_custom_call" | custom-call | tf_op jit(solution)/shard_map/outer_step/pallas_call | solution.py:283
  126.3 3.6 %write_out.1 = (f32[2,512,1792]{2,1,0:T(8,128)}, f32[2,32,4,1792]{3,2,1,0:T(4,128)}) custom-call(f32[2,512,1792]{2,1,0:T(8,128)S(1)} %get-tuple-element.6.new_w, f32[2,32,4,1792]{3,2,1,0:T(4,128)S(1)} %get-tuple-element.7.new_mom), custom_call_target="tpu_custom_call" | custom-call | tf_op jit(solution)/shard_map/write_out/pallas_call | solution.py:312

commit v4 on v3

--- a/solution.py
+++ b/solution.py
@@ -240,21 +240,30 @@
             relay_copy(direction, c, source, a).start()
     loop(CHUNKS, pass_on)
 
-    def drain(c):
-        for direction, near_a, a in ((UP, 1, 0), (DOWN, 0, 1)):
-            own_copy(direction, OUT_NEAR, c, near_a).wait_recv()
-            relay_copy(direction, c, far, a).wait_recv()
-        for direction in (UP, DOWN):
-            for kind in (FAR, NEAR, RELAY, OUT_FAR, OUT_NEAR, OUT_RELAY):
-                own_copy(direction, kind, c, 0).wait_send()
-    loop(CHUNKS, drain)
-
     def drain_plane(k):
         other = (me + k + 1) % plane
         in_copy(k + 1).wait_send()
         out_copy(other).wait_send()
         out_arrival(other).wait()
     loop(plane - 1, drain_plane)
+
+    def sent(c, *kinds):
+        for kind in kinds:
+            for direction in (UP, DOWN):
+                own_copy(direction, kind, c, 0).wait_send()
+
+    def arrived(c):
+        for direction, a in ((UP, 1), (DOWN, 0)):
+            own_copy(direction, OUT_NEAR, c, a).wait_recv()
+
+    loop(CHUNKS, lambda c: sent(c, FAR, NEAR, RELAY, OUT_FAR, OUT_NEAR))
+    loop(CHUNKS, arrived)
+
+    def drain(c):
+        sent(c, OUT_RELAY)
+        for direction, a in ((UP, 0), (DOWN, 1)):
+            relay_copy(direction, c, far, a).wait_recv()
+    loop(CHUNKS, drain)
 
 
 def write_out(new_w, new_mom, out_w, out_mom, sem):

time: 130 us -> 129 us (level)
  no operation moved by 1% of the time
where the time goes in v4:
time: 129 us
  Pallas kernels  129 us (100%)
    pallas_call x1, Pallas kernels, body(): pl.pallas_call(kernel, out_shape=(pltpu.VMEM(start_weights.shape, jnp.flo...  125 us
    pallas_call x1, Pallas kernels, body(): pl.pallas_call(write_out, out_shape=(jax.ShapeDtypeStruct(start_weights.s...  3.59 us

profile of v4, /device:TPU:1, one launch (start us, length us, event | category | flops | bytes accessed | tf_op | source)
XLA Modules:
  0.0 129.3 jit_solution(15241673323892885216)
XLA Ops:
  0.6 125.1 %outer_step.1 = (f32[2,512,1792]{2,1,0:T(8,128)S(1)}, f32[2,32,4,1792]{3,2,1,0:T(4,128)S(1)}) custom-call(f32[2,512,1792]{2,1,0:T(8,128)} %bitcast.5, f32[2,512,1792]{2,1,0:T(8,128)} %start.1, f32[2,32,4,1792]{3,2,1,0:T(4,128)} %bitcast.6), custom_call_target="tpu_custom_call" | custom-call | tf_op jit(solution)/shard_map/outer_step/pallas_call | solution.py:292
  125.8 3.6 %write_out.1 = (f32[2,512,1792]{2,1,0:T(8,128)}, f32[2,32,4,1792]{3,2,1,0:T(4,128)}) custom-call(f32[2,512,1792]{2,1,0:T(8,128)S(1)} %get-tuple-element.6.new_w, f32[2,32,4,1792]{3,2,1,0:T(4,128)S(1)} %get-tuple-element.7.new_mom), custom_call_target="tpu_custom_call" | custom-call | tf_op jit(solution)/shard_map/write_out/pallas_call | solution.py:321

commit v5 on v4

--- a/solution.py
+++ b/solution.py
@@ -18,7 +18,7 @@
 def kernel(
     inner, start, mom, new_w, new_mom,
     diff, base, land, mom_in, mom_out,
-    load_sem, z_send, z_recv, in_send, in_recv, out_send, out_recv, local_sem, near_sem, word_sem,
+    load_sem, z_send, z_recv, plane_sem, local_sem, near_sem, word_sem,
 ):
     groups, shards, tps = lax.axis_size("grp"), lax.axis_size("shard"), lax.axis_size("tp")
     plane = shards * tps
@@ -55,7 +55,7 @@
     def z_copy(direction, kind, c, src, dst):
         return pltpu.make_async_remote_copy(
             src_ref=src, dst_ref=dst,
-            send_sem=z_send.at[direction, kind, c], recv_sem=z_recv.at[direction, kind, c],
+            send_sem=z_send.at[direction], recv_sem=z_recv.at[direction, kind, c],
             device_id=side[direction], device_id_type=MESH)
 
     def sum_copy(direction, kind, c, quarter, a):
@@ -79,20 +79,20 @@
         other, device = partner(k)
         return pltpu.make_async_remote_copy(
             src_ref=mom.at[:, other], dst_ref=mom_in.at[:, me],
-            send_sem=in_send.at[other], recv_sem=in_recv.at[me],
+            send_sem=plane_sem.at[0], recv_sem=plane_sem.at[1],
             device_id=device, device_id_type=MESH)
 
-    def in_arrival(other):
-        return pltpu.make_async_copy(mom_in.at[:, other], mom_in.at[:, other], in_recv.at[other])
+    def wait_all(ref, sem):
+        pltpu.make_async_copy(ref, ref, sem).wait()
+
+    def wait_plane(i):
+        wait_all(mom_out.at[:, pl.ds(0, plane - 1)], plane_sem.at[i])
 
     def out_copy(other):
         return pltpu.make_async_remote_copy(
             src_ref=mom_out.at[:, other], dst_ref=new_mom.at[:, me],
-            send_sem=out_send.at[other], recv_sem=out_recv.at[me],
+            send_sem=plane_sem.at[2], recv_sem=plane_sem.at[3],
             device_id=(g, other // tps, other % tps), device_id_type=MESH)
-
-    def out_arrival(other):
-        return pltpu.make_async_copy(new_mom.at[:, other], new_mom.at[:, other], out_recv.at[other])
 
     def loop(n, body):
         def one(i, carry):
@@ -199,7 +199,7 @@
     loop(CHUNKS, send_relay)
 
     own_in.wait()
-    loop(plane - 1, lambda k: in_arrival((me + k + 1) % plane).wait())
+    wait_plane(1)
 
     def finish(c):
         for direction, near_a, relay_a in ((UP, 1, 0), (DOWN, 0, 1)):
@@ -240,30 +240,23 @@
             relay_copy(direction, c, source, a).start()
     loop(CHUNKS, pass_on)
 
-    def drain_plane(k):
-        other = (me + k + 1) % plane
-        in_copy(k + 1).wait_send()
-        out_copy(other).wait_send()
-        out_arrival(other).wait()
-    loop(plane - 1, drain_plane)
-
-    def sent(c, *kinds):
-        for kind in kinds:
-            for direction in (UP, DOWN):
-                own_copy(direction, kind, c, 0).wait_send()
+    wait_plane(0)
+    wait_plane(2)
+    wait_plane(3)
 
     def arrived(c):
         for direction, a in ((UP, 1), (DOWN, 0)):
             own_copy(direction, OUT_NEAR, c, a).wait_recv()
 
-    loop(CHUNKS, lambda c: sent(c, FAR, NEAR, RELAY, OUT_FAR, OUT_NEAR))
     loop(CHUNKS, arrived)
 
-    def drain(c):
-        sent(c, OUT_RELAY)
+    def passed_on(c):
         for direction, a in ((UP, 0), (DOWN, 1)):
             relay_copy(direction, c, far, a).wait_recv()
-    loop(CHUNKS, drain)
+    loop(CHUNKS, passed_on)
+
+    for direction in (UP, DOWN):
+        wait_all(new_w.at[:, pl.ds(0, 3 * rows)], z_send.at[direction])
 
 
 def write_out(new_w, new_mom, out_w, out_mom, sem):
@@ -304,12 +297,9 @@
             pltpu.VMEM(flat_shape, jnp.float32),
             pltpu.VMEM(flat_shape, jnp.float32),
             dma((4, 2)),
+            dma((2,)),
             dma((2, 6, CHUNKS)),
-            dma((2, 6, CHUNKS)),
-            dma((plane,)),
-            dma((plane,)),
-            dma((plane,)),
-            dma((plane,)),
+            dma((4,)),
             dma((1,)),
             pltpu.SemaphoreType.REGULAR((2,)),
             pltpu.SemaphoreType.REGULAR((7,)),

time: 129 us -> 128 us (level)
  Pallas kernels: 129 us -> 127 us
    pallas_call x1, Pallas kernels: 125 us -> 124 us  [body(): pl.pallas_call(kernel, out_shape=(pltpu.VMEM(start_weights.shape, jnp.flo...]
where the time goes in v5:
time: 128 us
  Pallas kernels  127 us (99%)
    pallas_call x1, Pallas kernels, body(): pl.pallas_call(kernel, out_shape=(pltpu.VMEM(start_weights.shape, jnp.flo...  124 us
    pallas_call x1, Pallas kernels, body(): pl.pallas_call(write_out, out_shape=(jax.ShapeDtypeStruct(start_weights.s...  3.59 us

profile of v5, /device:TPU:1, one launch (start us, length us, event | category | flops | bytes accessed | tf_op | source)
XLA Modules:
  0.0 128.0 jit_solution(10996006242868517421)
XLA Ops:
  0.6 123.8 %outer_step.1 = (f32[2,512,1792]{2,1,0:T(8,128)S(1)}, f32[2,32,4,1792]{3,2,1,0:T(4,128)S(1)}) custom-call(f32[2,512,1792]{2,1,0:T(8,128)} %bitcast.5, f32[2,512,1792]{2,1,0:T(8,128)} %start.1, f32[2,32,4,1792]{3,2,1,0:T(4,128)} %bitcast.6), custom_call_target="tpu_custom_call" | custom-call | tf_op jit(solution)/shard_map/outer_step/pallas_call | solution.py:285
  124.4 3.6 %write_out.1 = (f32[2,512,1792]{2,1,0:T(8,128)}, f32[2,32,4,1792]{3,2,1,0:T(4,128)}) custom-call(f32[2,512,1792]{2,1,0:T(8,128)S(1)} %get-tuple-element.6.new_w, f32[2,32,4,1792]{3,2,1,0:T(4,128)S(1)} %get-tuple-element.7.new_mom), custom_call_target="tpu_custom_call" | custom-call | tf_op jit(solution)/shard_map/write_out/pallas_call | solution.py:311

commit v6 on v5

--- a/solution.py
+++ b/solution.py
@@ -11,14 +11,14 @@
 MOMENTUM_COEF = 0.5
 CHUNKS = 2
 UP, DOWN = 0, 1
-FAR, NEAR, RELAY, OUT_FAR, OUT_NEAR, OUT_RELAY = range(6)
+FAR, NEAR, RELAY, OUT_FAR, OUT_END = 0, 1, 2, 2 + CHUNKS, 2 + 2 * CHUNKS
 MESH = pl.DeviceIdType.MESH
 
 
 def kernel(
     inner, start, mom, new_w, new_mom,
     diff, base, land, mom_in, mom_out,
-    load_sem, z_send, z_recv, plane_sem, local_sem, near_sem, word_sem,
+    load_sem, z_send, z_recv, plane_sem, near_sem, word_sem,
 ):
     groups, shards, tps = lax.axis_size("grp"), lax.axis_size("shard"), lax.axis_size("tp")
     plane = shards * tps
@@ -37,11 +37,11 @@
     def in_chunk(c):
         return pl.ds(pl.multiple_of(c * step, step), step)
 
-    def load(slot, a, quarter, begin):
-        where = pl.ds(pl.multiple_of(quarter * rows, rows), rows)
-        for k, (src, dst) in enumerate(((inner, diff), (start, base))):
-            copy = pltpu.make_async_copy(src.at[a, where], dst.at[a, where], load_sem.at[slot, k])
-            copy.start() if begin else copy.wait()
+    def whole(quarter):
+        return pl.ds(pl.multiple_of(quarter * rows, rows), rows)
+
+    def wait_all(ref, sem):
+        pltpu.make_async_copy(ref, ref, sem).wait()
 
     blocks = ((0, up), (1, down), (0, g), (1, g))
 
@@ -52,24 +52,26 @@
             return carry
         lax.fori_loop(0, CHUNKS, one, 0)
 
-    def z_copy(direction, kind, c, src, dst):
+    def z_copy(direction, slot, src, dst):
         return pltpu.make_async_remote_copy(
             src_ref=src, dst_ref=dst,
-            send_sem=z_send.at[direction], recv_sem=z_recv.at[direction, kind, c],
+            send_sem=z_send.at[direction], recv_sem=z_recv.at[direction, slot],
             device_id=side[direction], device_id_type=MESH)
 
-    def sum_copy(direction, kind, c, quarter, a):
-        source = diff if kind == RELAY else inner
-        slot = land.at[direction, kind, in_chunk(c)]
-        return z_copy(direction, kind, c, source.at[a, at_rows(quarter, c)], slot)
-
-    def own_copy(direction, kind, c, a):
+    def raw_copy(direction, kind, quarter, a):
+        return z_copy(direction, kind, inner.at[a, whole(quarter)], land.at[direction, kind])
+
+    def sum_copy(direction, c, quarter, a):
+        slot = land.at[direction, RELAY, in_chunk(c)]
+        return z_copy(direction, RELAY + c, diff.at[a, at_rows(quarter, c)], slot)
+
+    def far_copy(direction, c, a):
         where = at_rows(g, c)
-        return z_copy(direction, kind, c, new_w.at[a, where], new_w.at[a, where])
-
-    def relay_copy(direction, c, quarter, a):
-        where = at_rows(quarter, c)
-        return z_copy(direction, OUT_RELAY, c, new_w.at[a, where], new_w.at[a, where])
+        return z_copy(direction, OUT_FAR + c, new_w.at[a, where], new_w.at[a, where])
+
+    def end_copy(direction, quarter, a):
+        where = whole(quarter)
+        return z_copy(direction, OUT_END, new_w.at[a, where], new_w.at[a, where])
 
     def partner(k):
         other = (me + k) % plane
@@ -82,9 +84,6 @@
             send_sem=plane_sem.at[0], recv_sem=plane_sem.at[1],
             device_id=device, device_id_type=MESH)
 
-    def wait_all(ref, sem):
-        pltpu.make_async_copy(ref, ref, sem).wait()
-
     def wait_plane(i):
         wait_all(mom_out.at[:, pl.ds(0, plane - 1)], plane_sem.at[i])
 
@@ -119,26 +118,28 @@
     def _():
         signal(barrier, *side, *along_x, *along_y, *beside)
 
+    pl.semaphore_wait(barrier, jnp.where(g == 0, 5, jnp.where(g == 2, 2, 1)))
+
+
+    @pl.when((g == 3) | (g == 2))
+    def _():
+        signal(near_sem.at[DOWN], side[UP])
+
+    @pl.when((g == 1) | (g == 2))
+    def _():
+        signal(near_sem.at[UP], side[DOWN])
+
+    @pl.when(g == 3)
+    def _():
+        signal(barrier, side[DOWN])
+
     @pl.when(g == 1)
     def _():
         signal(barrier, side[UP])
 
-    @pl.when(g == 3)
-    def _():
-        signal(barrier, side[DOWN])
-    pl.semaphore_wait(barrier, jnp.where(g == 0, 5, jnp.where(g == 2, 2, 1)))
-
-    @pl.when((g == 1) | (g == 2))
-    def _():
-        signal(near_sem.at[UP], side[DOWN])
-
-    @pl.when((g == 3) | (g == 2))
-    def _():
-        signal(near_sem.at[DOWN], side[UP])
-
     def send_raw(direction, a, owner):
-        loop(CHUNKS, lambda c: sum_copy(direction, FAR, c, far, a).start())
-        loop(CHUNKS, lambda c: sum_copy(direction, NEAR, c, owner, 1 - a).start())
+        raw_copy(direction, FAR, far, a).start()
+        raw_copy(direction, NEAR, owner, 1 - a).start()
 
     @pl.when(g == 1)
     def _():
@@ -172,16 +173,16 @@
             else:
                 signal(word_sem.at[i + 1], (up, s, t), (far, s, t), (down, s, t))
 
-    for slot in range(4):
-        load(slot, *blocks[slot], True)
-    own_in = pltpu.make_async_copy(mom.at[:, me], mom_in.at[:, me], local_sem.at[0])
-    own_in.start()
+    for a, quarter in blocks:
+        for src, dst in ((inner, diff), (start, base)):
+            pltpu.make_async_copy(src.at[a, whole(quarter)], dst.at[a, whole(quarter)], load_sem).start()
+    pltpu.make_async_copy(mom.at[:, me], mom_in.at[:, me], plane_sem.at[1]).start()
 
     hear(0)
-    for slot in range(4):
-        load(slot, *blocks[slot], False)
-        subtract(*blocks[slot])
-        hear(slot + 1)
+    wait_all(base, load_sem)
+    for i in range(4):
+        subtract(*blocks[i])
+        hear(i + 1)
     hear(5)
 
     @pl.when(g != 0)
@@ -189,22 +190,24 @@
         pl.semaphore_wait(word_sem.at[6], 1)
     loop(plane - 1, lambda k: in_copy(k + 1).start())
 
-    def send_relay(c):
+    for direction, a in ((UP, 0), (DOWN, 1)):
+        raw_copy(direction, FAR, far, a).wait_recv()
+
+    def send_sums(c):
         for direction, a, quarter in ((UP, 0, up), (DOWN, 1, down)):
-            sum_copy(direction, FAR, c, far, a).wait_recv()
             where = at_rows(quarter, c)
             diff[a, where] = diff[a, where] + (base[a, where] - land[direction, FAR, in_chunk(c)])
-        sum_copy(UP, RELAY, c, up, 0).start()
-        sum_copy(DOWN, RELAY, c, down, 1).start()
-    loop(CHUNKS, send_relay)
-
-    own_in.wait()
-    wait_plane(1)
+        sum_copy(UP, c, up, 0).start()
+        sum_copy(DOWN, c, down, 1).start()
+    loop(CHUNKS, send_sums)
+
+    wait_all(mom_in, plane_sem.at[1])
+    for direction, a in ((UP, 1), (DOWN, 0)):
+        raw_copy(direction, NEAR, far, a).wait_recv()
 
     def finish(c):
-        for direction, near_a, relay_a in ((UP, 1, 0), (DOWN, 0, 1)):
-            sum_copy(direction, NEAR, c, up, near_a).wait_recv()
-            sum_copy(direction, RELAY, c, up, relay_a).wait_recv()
+        for direction, a in ((UP, 0), (DOWN, 1)):
+            sum_copy(direction, c, up, a).wait_recv()
 
         def pair(i):
             for a, near, relay in ((0, DOWN, UP), (1, UP, DOWN)):
@@ -219,10 +222,8 @@
                 mom_out[a, j + 1] = fresh[q_rows:]
                 new_w[a, where] = base[a, where] - OUTER_RATE * (flat + MOMENTUM_COEF * fresh)
         loop(per_step // 2, pair)
-        own_copy(UP, OUT_FAR, c, 0).start()
-        own_copy(DOWN, OUT_FAR, c, 1).start()
-        own_copy(UP, OUT_NEAR, c, 1).start()
-        own_copy(DOWN, OUT_NEAR, c, 0).start()
+        far_copy(UP, c, 0).start()
+        far_copy(DOWN, c, 1).start()
 
         def give(i):
             other = c * per_step + i
@@ -232,29 +233,20 @@
                 out_copy(other).start()
         loop(per_step, give)
     loop(CHUNKS, finish)
+    end_copy(UP, g, 1).start()
+    end_copy(DOWN, g, 0).start()
     new_mom[:, me] = mom_out[:, me]
 
-    def pass_on(c):
-        for direction, source, a in ((UP, down, 0), (DOWN, up, 1)):
-            own_copy(direction, OUT_FAR, c, a).wait_recv()
-            relay_copy(direction, c, source, a).start()
-    loop(CHUNKS, pass_on)
+    for direction, source, a in ((UP, down, 0), (DOWN, up, 1)):
+        loop(CHUNKS, lambda c: far_copy(direction, c, a).wait_recv())
+        end_copy(direction, source, a).start()
 
     wait_plane(0)
     wait_plane(2)
     wait_plane(3)
 
-    def arrived(c):
-        for direction, a in ((UP, 1), (DOWN, 0)):
-            own_copy(direction, OUT_NEAR, c, a).wait_recv()
-
-    loop(CHUNKS, arrived)
-
-    def passed_on(c):
-        for direction, a in ((UP, 0), (DOWN, 1)):
-            relay_copy(direction, c, far, a).wait_recv()
-    loop(CHUNKS, passed_on)
-
+    for direction in (UP, DOWN):
+        wait_all(new_w.at[:, whole(0)], z_recv.at[direction, OUT_END])
     for direction in (UP, DOWN):
         wait_all(new_w.at[:, pl.ds(0, 3 * rows)], z_send.at[direction])
 
@@ -296,11 +288,10 @@
             pltpu.VMEM((2, 3, quarter, col_count), jnp.float32),
             pltpu.VMEM(flat_shape, jnp.float32),
             pltpu.VMEM(flat_shape, jnp.float32),
-            dma((4, 2)),
+            dma,
             dma((2,)),
-            dma((2, 6, CHUNKS)),
+            dma((2, 3 + 2 * CHUNKS)),
             dma((4,)),
-            dma((1,)),
             pltpu.SemaphoreType.REGULAR((2,)),
             pltpu.SemaphoreType.REGULAR((7,)),
         ],

time: 128 us -> 128 us (level)
  no operation moved by 1% of the time
where the time goes in v6:
time: 128 us
  Pallas kernels  127 us (99%)
    pallas_call x1, Pallas kernels, body(): pl.pallas_call(kernel, out_shape=(pltpu.VMEM(start_weights.shape, jnp.flo...  124 us
    pallas_call x1, Pallas kernels, body(): pl.pallas_call(write_out, out_shape=(jax.ShapeDtypeStruct(start_weights.s...  3.59 us

profile of v6, /device:TPU:1, one launch (start us, length us, event | category | flops | bytes accessed | tf_op | source)
XLA Modules:
  0.0 127.9 jit_solution(10137008491871212517)
XLA Ops:
  0.6 123.6 %outer_step.1 = (f32[2,512,1792]{2,1,0:T(8,128)S(1)}, f32[2,32,4,1792]{3,2,1,0:T(4,128)S(1)}) custom-call(f32[2,512,1792]{2,1,0:T(8,128)} %bitcast.5, f32[2,512,1792]{2,1,0:T(8,128)} %start.1, f32[2,32,4,1792]{3,2,1,0:T(4,128)} %bitcast.6), custom_call_target="tpu_custom_call" | custom-call | tf_op jit(solution)/shard_map/outer_step/pallas_call | solution.py:277
  124.3 3.6 %write_out.1 = (f32[2,512,1792]{2,1,0:T(8,128)}, f32[2,32,4,1792]{3,2,1,0:T(4,128)}) custom-call(f32[2,512,1792]{2,1,0:T(8,128)S(1)} %get-tuple-element.6.new_w, f32[2,32,4,1792]{3,2,1,0:T(4,128)S(1)} %get-tuple-element.7.new_mom), custom_call_target="tpu_custom_call" | custom-call | tf_op jit(solution)/shard_map/write_out/pallas_call | solution.py:302

commit v7 on v6

--- a/solution.py
+++ b/solution.py
@@ -9,7 +9,7 @@
 
 OUTER_RATE = 0.7
 MOMENTUM_COEF = 0.5
-CHUNKS = 2
+CHUNKS = 4
 UP, DOWN = 0, 1
 FAR, NEAR, RELAY, OUT_FAR, OUT_END = 0, 1, 2, 2 + CHUNKS, 2 + 2 * CHUNKS
 MESH = pl.DeviceIdType.MESH

time: 128 us -> 128 us (level)
  no operation moved by 1% of the time
where the time goes in v7:
time: 128 us
  Pallas kernels  127 us (99%)
    pallas_call x1, Pallas kernels, body(): pl.pallas_call(kernel, out_shape=(pltpu.VMEM(start_weights.shape, jnp.flo...  124 us
    pallas_call x1, Pallas kernels, body(): pl.pallas_call(write_out, out_shape=(jax.ShapeDtypeStruct(start_weights.s...  3.59 us

profile of v7, /device:TPU:1, one launch (start us, length us, event | category | flops | bytes accessed | tf_op | source)
XLA Modules:
  0.0 127.9 jit_solution(17267562642269674568)
XLA Ops:
  0.6 123.7 %outer_step.1 = (f32[2,512,1792]{2,1,0:T(8,128)S(1)}, f32[2,32,4,1792]{3,2,1,0:T(4,128)S(1)}) custom-call(f32[2,512,1792]{2,1,0:T(8,128)} %bitcast.5, f32[2,512,1792]{2,1,0:T(8,128)} %start.1, f32[2,32,4,1792]{3,2,1,0:T(4,128)} %bitcast.6), custom_call_target="tpu_custom_call" | custom-call | tf_op jit(solution)/shard_map/outer_step/pallas_call | solution.py:277
  124.4 3.6 %write_out.1 = (f32[2,512,1792]{2,1,0:T(8,128)}, f32[2,32,4,1792]{3,2,1,0:T(4,128)}) custom-call(f32[2,512,1792]{2,1,0:T(8,128)S(1)} %get-tuple-element.6.new_w, f32[2,32,4,1792]{3,2,1,0:T(4,128)S(1)} %get-tuple-element.7.new_mom), custom_call_target="tpu_custom_call" | custom-call | tf_op jit(solution)/shard_map/write_out/pallas_call | solution.py:302
